TPU v7x, 512 devices: a whole 4x4x16 slice. The times are simulated.
512 devices in a mesh: seg: 64 (over z, x), sub: 8 (over y, core).
Axes of the slice: x: 4, y: 4, z: 16, core: 2. Of those that a mesh axis runs over, the one named last changes fastest.
Arguments:
- near_blocks: bfloat16 [1024, 10, 256, 256], P(('seg', 'sub')), may hold values from -0.375 to 0.375
- sample_cols: bfloat16 [262144, 256], P(('seg', 'sub')), may hold values from -6 to 6
- near_list: int32 [1024, 10], P(('seg', 'sub')), may hold values from -1 to 1023, as said below
- row_basis_t: bfloat16 [1024, 64, 256], P(('seg', 'sub')), may hold values from -0.75 to 0.75
- col_basis_t: bfloat16 [1024, 64, 256], P(('seg', 'sub')), may hold values from -0.375 to 0.375
- couplings: bfloat16 [64, 8, 64, 64, 128], P('seg', 'sub'), may hold values from -0.125 to 0.125
- far_source: int32 [64, 8, 64, 2], P('seg', 'sub'), may hold values from 0 to 2
- far_dest: int32 [64, 8, 64, 2], P('seg', 'sub'), may hold values from 0 to 1
Outputs:
- samples: bfloat16 [262144, 256], P(('seg', 'sub'))
- segment_factor: float32 [16384, 256], P('seg')
- transfers: bfloat16 [64, 3, 256, 256], P('seg')
Inputs may be any that keep to these rules, and one draw needn't show every extreme that they name: `near_list`: entry 0 of every list is the leaf itself; -1 marks padding and stands only after the real entries; every other entry names a leaf held by the same device or by the device just before or just after it in the order of seg, then sub. `far_source`: entry [s', u, s, c] is the local leaf of device (s', u) whose far projection fills slot c toward device (s, u); the value 2 marks an empty slot. `far_dest`: entry [s, u, s', c] is the local leaf of device (s, u) that slot c from device (s', u) serves.
All inputs are finite; a program needn't handle non-finite values.
Results may differ from a plain program's by a relative error of at most 0.013.
Values may be sent and summed in bfloat16 or wider, within the bound.
A program may use at most 64 MiB of HBM per device.

v0:
```python
import jax
import jax.numpy as jnp
from jax import lax
from jax.sharding import PartitionSpec as P

LEVELS = 3


def padded(value, sides, width):
    for axis, dim in sides:
        size, length = (lax.axis_size(axis), value.shape[dim])
        up = [(i, (i + 1) % size) for i in range(size - 1)]
        down = [(j, i) for i, j in up]
        last = lax.slice_in_dim(value, length - width, length, axis=dim)
        leading = lax.slice_in_dim(value, 0, width, axis=dim)
        before = lax.ppermute(last, axis, up)
        after = lax.ppermute(leading, axis, down)
        value = jnp.concatenate([before, value, after], axis=dim)
    return value


def from_partner(value, axis, distance):
    mask = 2**distance
    pairs = [(source, source ^ mask) for source in range(lax.axis_size(axis))]
    return lax.ppermute(value, axis, pairs)


def body(
    near_blocks, sample_cols, near_list, row_basis_t, col_basis_t, couplings, far_source, far_dest
):
    leaf_count, near_count, leaf_rows, _ = near_blocks.shape
    sample_width = sample_cols.shape[1]
    rank_width = row_basis_t.shape[1]
    seg_count = lax.axis_size("seg")
    slot_number_count = far_source.shape[3]
    random_cols = sample_cols.reshape(leaf_count, leaf_rows, sample_width)
    basis_projector = jnp.einsum(
        "jra,jas->jrs", col_basis_t, random_cols, preferred_element_type=jnp.float32
    ).astype(jnp.bfloat16)
    extended = padded(sample_cols, ((("seg", "sub"), 0),), leaf_count * leaf_rows)
    extended = extended.reshape(3 * leaf_count, leaf_rows, sample_width)
    base_leaf = (lax.axis_index(("seg", "sub")) - 1) * leaf_count
    usable = near_list >= 0
    position = jnp.where(usable, near_list - base_leaf, 0)
    chosen = extended[position]
    chosen = jnp.where(usable[:, :, None, None], chosen, jnp.zeros_like(chosen))
    near_part = jnp.einsum(
        "lkab,lkbs->las", near_blocks, chosen, preferred_element_type=jnp.float32
    )
    leaf_range = jnp.arange(leaf_count, dtype=jnp.int32)
    routing = far_dest[0, 0][:, :, None] == leaf_range[None, None, :]
    coupling_set = jnp.transpose(
        couplings[0, 0].reshape(seg_count, rank_width, slot_number_count, rank_width), (1, 0, 2, 3)
    )
    masked = jnp.where(
        jnp.transpose(routing, (2, 0, 1))[:, None, :, :, None],
        coupling_set[None],
        jnp.zeros((), jnp.bfloat16),
    )
    masked = masked.reshape(leaf_count * rank_width, seg_count * slot_number_count * rank_width)
    selection_choice = (far_source[0, 0][:, :, None] == leaf_range[None, None, :]).astype(
        jnp.bfloat16
    )
    outgoing = jnp.einsum(
        "zgy,ykf->zgkf", selection_choice, basis_projector, preferred_element_type=jnp.float32
    ).astype(jnp.bfloat16)
    incoming = lax.all_to_all(outgoing, "seg", split_axis=0, concat_axis=0, tiled=True)
    far_total = jnp.dot(
        masked,
        incoming.reshape(seg_count * slot_number_count * rank_width, sample_width),
        preferred_element_type=jnp.float32,
    )
    far_coeff = far_total.astype(jnp.bfloat16).reshape(leaf_count, rank_width, sample_width)
    distant_portion = jnp.einsum(
        "lra,lrs->las", row_basis_t, far_coeff, preferred_element_type=jnp.float32
    )
    samples = (
        (near_part + distant_portion)
        .astype(jnp.bfloat16)
        .reshape(leaf_count * leaf_rows, sample_width)
    )
    gram_local = lax.dot_general(
        samples, samples, (((0,), (0,)), ((), ())), preferred_element_type=jnp.float32
    )
    row_total = lax.axis_size("sub") * leaf_count * leaf_rows
    current = lax.psum(gram_local.astype(jnp.bfloat16), "sub").astype(jnp.float32) / row_total
    gram_levels = [current]
    for segment_position_index in range(LEVELS):
        partner = from_partner(current.astype(jnp.bfloat16), "seg", segment_position_index).astype(
            current.dtype
        )
        current = (current + partner) * 0.5
        gram_levels.append(current)
    stacked = jnp.stack(gram_levels)
    triangles = jnp.linalg.cholesky(stacked)
    segment_factor = jnp.swapaxes(triangles[0], 0, 1)
    solved = jax.vmap(
        lambda upper_one, lower_one: jax.scipy.linalg.solve_triangular(
            upper_one, lower_one, lower=True
        )
    )(triangles[1:], triangles[:-1])
    transfers = jnp.swapaxes(solved, 1, 2).astype(jnp.bfloat16)[None]
    return (samples, segment_factor, transfers)


def solution(mesh):
    in_specs = (
        P(("seg", "sub"), None, None, None),
        P(("seg", "sub"), None),
        P(("seg", "sub"), None),
        P(("seg", "sub"), None, None),
        P(("seg", "sub"), None, None),
        P("seg", "sub", None, None, None),
        P("seg", "sub", None, None),
        P("seg", "sub", None, None),
    )
    out_specs = (P(("seg", "sub"), None), P("seg", None), P("seg", None, None, None))
    return jax.shard_map(body, mesh=mesh, in_specs=in_specs, out_specs=out_specs, check_vma=False)
```

profile of v0, /device:TPU:2, one launch (start us, length us, event | category | flops | bytes accessed | tf_op | source)
XLA Modules:
  0.0 559.7 jit_solution(11103013563132528204)
XLA Ops:
  7.2 1.3 convolution_convert_fusion.3
  8.5 2.0 convolution_convert_fusion
  10.5 4.4 copy.66
  14.9 19.0 %all-to-all-start = ((bf16[64,2,64,256]{3,2,1,0:T(8,128)(2,1)}), bf16[64,2,64,256]{3,2,1,0:T(8,128)(2,1)}, u32[]{:S(2)}, u32[]{:S(2)}) async-start(bf16[64,2,64,256]{3,2,1,0:T(8,128)(2,1)} %copy.66), calls=%async_computation | async-start | bytes 8388608 | tf_op jit(solution)/shard_map/all_to_all | solution.py:67
  33.9 1.9 collective-permute-start
  35.8 5.8 %collective-permute-start.1 = (bf16[512,256]{1,0:T(8,128)(2,1)S(1)}, bf16[512,256]{1,0:T(8,128)(2,1)}, u32[]{:S(2)}, u32[]{:S(2)}) collective-permute-start(bf16[512,256]{1,0:T(8,128)(2,1)S(1)} %copy-done.4), channel_id=1, source_target_pairs={{1,0},{2,1},{3,2},{4,3},{5,4},{6,5},{7,6},{8,7},{9,8},{10,9},{11,1... | collective-permute-start | bytes 786440 | tf_op jit(solution)/shard_map/ppermute | solution.py:17
  41.7 5.3 reshape_squeeze.3
  47.1 4.0 copy.95
  51.1 2.3 broadcast_select_fusion
  53.4 12.6 %copy.64 = bf16[2,64,64,2,64]{4,3,2,1,0:T(2,128)(2,1)} copy(bf16[2,64,64,2,64]{4,2,3,1,0:T(8,128)(2,1)} %broadcast_select_fusion) | data formatting | bytes 4194304 | tf_op jit(solution)/shard_map/jit(_where)/select_n | solution.py:55
  66.0 21.4 %select_n.33 = bf16[128,8192]{1,0:T(8,128)(2,1)} reshape(bf16[2,64,64,2,64]{4,3,2,1,0:T(2,128)(2,1)} %copy.64) | data formatting | bytes 4194304 | tf_op jit(solution)/shard_map/jit(_where)/select_n | solution.py:55
  88.1 1.2 pad_maximum_fusion.1
  89.3 2.4 gather_fusion
  91.7 2.6 fusion.4
  94.4 129.4 %all-to-all-done = bf16[64,2,64,256]{3,2,1,0:T(8,128)(2,1)} async-done(((bf16[64,2,64,256]{3,2,1,0:T(8,128)(2,1)}), bf16[64,2,64,256]{3,2,1,0:T(8,128)(2,1)}, u32[]{:S(2)}, u32[]{:S(2)}) %all-to-all-start) | async-done | bytes 4194336 | tf_op jit(solution)/shard_map/all_to_all | solution.py:67
  223.8 3.6 convolution_convert_fusion.2
  228.3 0.9 fusion.8
  229.3 76.0 %all-reduce.3.cloned.1.call-done = bf16[256,256]{0,1:T(8,128)(2,1)} async-done(((bf16[256,256]{0,1:T(8,128)(2,1)}), bf16[256,256]{0,1:T(8,128)(2,1)}) %all-reduce.3.cloned.1.call-update) | async-done | bytes 131088 | tf_op jit(solution)/shard_map/psum | solution.py:86
  305.3 0.9 fusion.16
  306.2 2.5 collective-permute-start.2
  308.7 4.4 collective-permute-done.2
  313.1 1.0 fusion.17
  314.1 4.0 collective-permute-start.3
  318.7 3.7 collective-permute-done.3
  322.4 1.0 fusion.29
  323.5 3.5 collective-permute-start.4
  328.1 2.3 collective-permute-done.4
  330.4 1.1 fusion.20
  332.3 1.1 pad_maximum_fusion
  333.3 2.5 copy.69
  335.9 1.4 fusion.9
  337.3 1.0 copy-done.2
  338.3 46.9 %custom-call.17 = f32[4,128,128]{2,1,0:T(8,128)S(1)} custom-call(f32[4,128,128]{2,1,0:T(8,128)S(1)} %cholesky.122), custom_call_target="Cholesky" | custom-call | tf_op jit(solution)/shard_map/jit(cholesky)/cholesky | solution.py:95
  385.2 1.1 cholesky.117
  386.3 39.3 %custom-call.18 = f32[4,1,128,128]{2,3,1,0:T(8,128)S(1)} custom-call(f32[4,1,128,128]{3,2,1,0:T(8,128)S(1)} %select_bitcast_fusion), custom_call_target="InvertDiagBlocksLowerTriangular" | custom-call | tf_op jit(solution)/shard_map/jit(cholesky)/cholesky | solution.py:95
  425.6 2.1 constant_dynamic-update-slice_fusion.1
  427.8 1.6 convolution_subtract_fusion.1
  429.4 46.9 %custom-call.19 = f32[4,128,128]{2,1,0:T(8,128)S(1)} custom-call(f32[4,128,128]{2,1,0:T(8,128)S(1)} %convolution_subtract_fusion.1), custom_call_target="Cholesky" | custom-call | tf_op jit(solution)/shard_map/jit(cholesky)/cholesky | solution.py:95
  477.2 1.4 select_select_fusion
  478.7 0.9 copy-done.1
  480.4 5.4 while.1
  481.0 2.1 bitcast_dynamic-update-slice_fusion.2
  483.7 2.1 bitcast_dynamic-update-slice_fusion.2
  485.8 60.4 %custom-call.20 = f32[3,2,128,128]{2,3,1,0:T(8,128)} custom-call(f32[3,2,128,128]{3,2,1,0:T(8,128)} %bitcast.101), custom_call_target="InvertDiagBlocksLowerTriangular" | custom-call | tf_op jit(solution)/shard_map/vmap(jit(_solve_triangular))/triangular_solve | solution.py:98
  546.2 1.7 fusion.31
  547.8 1.5 convolution_subtract_fusion
  549.9 0.9 copy.76
  550.8 1.8 copy.75
  (57 shorter events, 8.0 us)
Async XLA Ops:
  7.2 84.6 %copy-start = (bf16[2,10,256,256]{3,2,1,0:T(8,128)(2,1)S(1)}, bf16[2,10,256,256]{3,2,1,0:T(8,128)(2,1)}, u32[]{:S(2)}) copy-start(bf16[2,10,256,256]{3,2,1,0:T(8,128)(2,1)} %param.8) | copy-start | bytes 7864324
  14.9 19.0 %copy-start.4 = (bf16[512,256]{1,0:T(8,128)(2,1)S(1)}, bf16[512,256]{1,0:T(8,128)(2,1)}, u32[]{:S(2)}) copy-start(bf16[512,256]{1,0:T(8,128)(2,1)} %param.9) | copy-start | bytes 786436
  14.9 26.7 %copy-start.13 = (s32[2,10]{1,0:T(2,128)S(1)}, s32[2,10]{1,0:T(2,128)}, u32[]{:S(2)}) copy-start(s32[2,10]{1,0:T(2,128)} %param.10) | copy-start | bytes 244
  14.9 208.9 %all-to-all-start = ((bf16[64,2,64,256]{3,2,1,0:T(8,128)(2,1)}), bf16[64,2,64,256]{3,2,1,0:T(8,128)(2,1)}, u32[]{:S(2)}, u32[]{:S(2)}) async-start(bf16[64,2,64,256]{3,2,1,0:T(8,128)(2,1)} %copy.66), calls=%async_computation | async-start | bytes 8388608 | tf_op jit(solution)/shard_map/all_to_all | solution.py:67
  33.9 271.5 %all-reduce.3.cloned.1.call-start = ((), (), s32[]{:S(2)}) async-start(), calls=%async_computation.1 | async-start | bytes 262144 | tf_op jit(solution)/shard_map/psum | solution.py:86
  33.9 53.5 %collective-permute-start = (bf16[512,256]{1,0:T(8,128)(2,1)S(1)}, bf16[512,256]{1,0:T(8,128)(2,1)S(1)}, u32[]{:S(2)}, u32[]{:S(2)}) collective-permute-start(bf16[512,256]{1,0:T(8,128)(2,1)S(1)} %copy-done.4), channel_id=1, source_target_pairs={{0,1},{1,2},{2,3},{3,4},{4,5},{5,6},{6,7},{7,8},{8,9},{9,10},{10,1... | collective-permute-start | bytes 786440 | tf_op jit(solution)/shard_map/ppermute | solution.py:16
  35.8 52.3 %collective-permute-start.1 = (bf16[512,256]{1,0:T(8,128)(2,1)S(1)}, bf16[512,256]{1,0:T(8,128)(2,1)}, u32[]{:S(2)}, u32[]{:S(2)}) collective-permute-start(bf16[512,256]{1,0:T(8,128)(2,1)S(1)} %copy-done.4), channel_id=1, source_target_pairs={{1,0},{2,1},{3,2},{4,3},{5,4},{6,5},{7,6},{8,7},{9,8},{10,9},{11,1... | collective-permute-start | bytes 786440 | tf_op jit(solution)/shard_map/ppermute | solution.py:17
  47.1 4.0 copy-start.12
  87.4 0.7 copy-start.9
  223.8 3.6 copy-start.10
  227.6 0.7 copy-start.8
  306.2 6.9 %collective-permute-start.2 = (bf16[256,256]{0,1:T(8,128)(2,1)S(1)}, bf16[256,256]{0,1:T(8,128)(2,1)S(1)}, u32[]{:S(2)}, u32[]{:S(2)}) collective-permute-start(bf16[256,256]{0,1:T(8,128)(2,1)S(1)} %fusion.16), channel_id=1, source_target_pairs={{0,8},{8,0},{16,24},{24,16},{32,40},{40,32},{48,56},{56,48},{64,72... | collective-permute-start | bytes 393224 | tf_op jit(solution)/shard_map/ppermute | solution.py:25
  314.1 8.4 %collective-permute-start.3 = (bf16[256,256]{0,1:T(8,128)(2,1)S(1)}, bf16[256,256]{0,1:T(8,128)(2,1)S(1)}, u32[]{:S(2)}, u32[]{:S(2)}) collective-permute-start(bf16[256,256]{0,1:T(8,128)(2,1)S(1)} %get-tuple-element.44), channel_id=1, source_target_pairs={{0,16},{8,24},{16,0},{24,8},{32,48},{40,56},{48,32},{56,40},{64,80... | collective-permute-start | bytes 393224 | tf_op jit(solution)/shard_map/ppermute | solution.py:25
  322.4 5.7 %copy-start.6 = (bf16[256,256]{0,1:T(8,128)(2,1)}, bf16[256,256]{0,1:T(8,128)(2,1)S(1)}, u32[]{:S(2)}) copy-start(bf16[256,256]{0,1:T(8,128)(2,1)S(1)} %collective-permute-done.3) | copy-start | bytes 393220
  323.5 7.0 %collective-permute-start.4 = (bf16[256,256]{0,1:T(8,128)(2,1)S(1)}, bf16[256,256]{0,1:T(8,128)(2,1)}, u32[]{:S(2)}, u32[]{:S(2)}) collective-permute-start(bf16[256,256]{0,1:T(8,128)(2,1)S(1)} %get-tuple-element.39), channel_id=1, source_target_pairs={{0,32},{8,40},{16,48},{24,56},{32,0},{40,8},{48,16},{56,24},{64,96... | collective-permute-start | bytes 393224 | tf_op jit(solution)/shard_map/ppermute | solution.py:25
  331.6 0.7 copy-start.3
  335.9 50.4 %copy-start.11 = (pred[128,128]{1,0:T(8,128)(4,1)S(1)}, pred[128,128]{1,0:T(8,128)(4,1)}, u32[]{:S(2)}) copy-start(pred[128,128]{1,0:T(8,128)(4,1)} %iota_compare_fusion.1) | copy-start | bytes 49156
  337.3 1.0 copy-start.2
  338.3 138.9 %copy-start.5 = (pred[256,256]{1,0:T(8,128)(4,1)S(1)}, pred[256,256]{1,0:T(8,128)(4,1)}, u32[]{:S(2)}) copy-start(pred[256,256]{1,0:T(8,128)(4,1)} %iota_compare_fusion) | copy-start | bytes 196612
  429.4 51.0 %copy-start.14 = (s32[2]{0:T(128)S(1)}, s32[2]{0:T(128)}, u32[]{:S(2)}) copy-start(s32[2]{0:T(128)} %iota_multiply_fusion) | copy-start | bytes 28
  478.6 1.0 copy-start.1
  546.2 3.2 copy-start.7
Sparse Core Ops, SparseCore 0:
  229.4 75.8 all-reduce.2
where the time goes:
time: 566 us; the launch traced here: 560 us
  waiting for transfers between devices  216 us (38%)
  other arithmetic  208 us (37%)
  local copies, waits for them, and re-layouts  66.8 us (12%)
  starting transfers between devices  36.6 us (6%)
  matrix products  18.1 us (3%)
  between operations  14.6 us (3%)
    another operation x9, other arithmetic, body(): triangles = jnp.linalg.cholesky(stacked)  135 us
    all_to_all x1, waiting for transfers between devices, body(): lax.all_to_all(outgoing, 'seg', split_axis=0, concat_axis=0, tiled=True)  129 us
    psum x1, waiting for transfers between devices, body(): lax.psum(gram_local.astype(jnp.bfloat16), 'sub').astype(jnp.float32)  76 us
    another operation x3, other arithmetic, body(): jax.scipy.linalg.solve_triangular(upper_one, lower_one, lower=True)  61 us
    select_n x2, local copies, waits for them, and re-layouts, body(): jnp.where(jnp.transpose(routing, (2, 0, 1))[:, None, :, :, None], couplin...  34 us
    all_to_all x1, starting transfers between devices, body(): lax.all_to_all(outgoing, 'seg', split_axis=0, concat_axis=0, tiled=True)  19 us
  transfers between devices with their start and end apart: 7, of which 5 were waited for; matrix products, arithmetic and copies ran while one was open for 10% of the time, Pallas kernels for 0%

commit v1 on v0

--- a/solution.py
+++ b/solution.py
@@ -83,7 +83,8 @@
         samples, samples, (((0,), (0,)), ((), ())), preferred_element_type=jnp.float32
     )
     row_total = lax.axis_size("sub") * leaf_count * leaf_rows
-    current = lax.psum(gram_local.astype(jnp.bfloat16), "sub").astype(jnp.float32) / row_total
+    _remake_values = lambda shard_in: jnp.sum(lax.all_gather(shard_in, "sub"), axis=0)
+    current = _remake_values(gram_local.astype(jnp.bfloat16)).astype(jnp.float32) / row_total
     gram_levels = [current]
     for segment_position_index in range(LEVELS):
         partner = from_partner(current.astype(jnp.bfloat16), "seg", segment_position_index).astype(

time: 566 us -> 522 us (0.922)
  waiting for transfers between devices: 216 us -> 172 us
    psum x1 -> x0, waiting for transfers between devices: 76 us -> none  [body(): lax.psum(gram_local.astype(jnp.bfloat16), 'sub').astype(jnp.float32)]
    all_gather x0 -> x1, waiting for transfers between devices: none -> 31.5 us  [body(): lax.all_gather(shard_in, 'sub')]
where the time goes in v1:
time: 522 us; the launch traced here: 516 us
  other arithmetic  207 us (40%)
  waiting for transfers between devices  172 us (33%)
  local copies, waits for them, and re-layouts  67.6 us (13%)
  starting transfers between devices  36.8 us (7%)
  matrix products  18.1 us (3%)
  between operations  14.6 us (3%)
    another operation x9, other arithmetic, body(): triangles = jnp.linalg.cholesky(stacked)  135 us
    all_to_all x1, waiting for transfers between devices, body(): lax.all_to_all(outgoing, 'seg', split_axis=0, concat_axis=0, tiled=True)  129 us
    another operation x3, other arithmetic, body(): jax.scipy.linalg.solve_triangular(upper_one, lower_one, lower=True)  61 us
    select_n x2, local copies, waits for them, and re-layouts, body(): jnp.where(jnp.transpose(routing, (2, 0, 1))[:, None, :, :, None], couplin...  34.1 us
    all_gather x1, waiting for transfers between devices, body(): lax.all_gather(shard_in, 'sub')  31.5 us
    all_to_all x1, starting transfers between devices, body(): lax.all_to_all(outgoing, 'seg', split_axis=0, concat_axis=0, tiled=True)  19 us
    ppermute x3, waiting for transfers between devices, from_partner(): return lax.ppermute(value, axis, pairs)  10.9 us
  transfers between devices with their start and end apart: 7, of which 5 were waited for; matrix products, arithmetic and copies ran while one was open for 10% of the time, Pallas kernels for 0%

profile of v1, /device:TPU:2, one launch (start us, length us, event | category | flops | bytes accessed | tf_op | source)
XLA Modules:
  0.0 515.8 jit_solution(15624283908412215658)
XLA Ops:
  7.2 1.3 convolution_convert_fusion.3
  8.5 2.0 convolution_convert_fusion
  10.5 4.4 copy.64
  14.9 19.0 %all-to-all-start = ((bf16[64,2,64,256]{3,2,1,0:T(8,128)(2,1)}), bf16[64,2,64,256]{3,2,1,0:T(8,128)(2,1)}, u32[]{:S(2)}, u32[]{:S(2)}) async-start(bf16[64,2,64,256]{3,2,1,0:T(8,128)(2,1)} %copy.64), calls=%async_computation | async-start | bytes 8388608 | tf_op jit(solution)/shard_map/all_to_all | solution.py:67
  33.9 1.9 collective-permute-start
  35.8 5.8 %collective-permute-start.1 = (bf16[512,256]{1,0:T(8,128)(2,1)S(1)}, bf16[512,256]{1,0:T(8,128)(2,1)}, u32[]{:S(2)}, u32[]{:S(2)}) collective-permute-start(bf16[512,256]{1,0:T(8,128)(2,1)S(1)} %copy-done.5), channel_id=1, source_target_pairs={{1,0},{2,1},{3,2},{4,3},{5,4},{6,5},{7,6},{8,7},{9,8},{10,9},{11,1... | collective-permute-start | bytes 786440 | tf_op jit(solution)/shard_map/ppermute | solution.py:17
  41.7 5.3 %reshape_squeeze.3 = bf16[64,64,2,64]{3,2,1,0:T(2,128)(2,1)} reshape(bf16[1,1,64,64,128]{4,3,2,1,0:T(8,128)(2,1)} %param.13) | data formatting | bytes 2097152 | tf_op jit(solution)/shard_map/reshape;squeeze | solution.py:53
  47.1 4.0 copy.91
  51.1 2.3 broadcast_select_fusion
  53.4 12.6 %copy.62 = bf16[2,64,64,2,64]{4,3,2,1,0:T(2,128)(2,1)} copy(bf16[2,64,64,2,64]{4,2,3,1,0:T(8,128)(2,1)} %broadcast_select_fusion) | data formatting | bytes 4194304 | tf_op jit(solution)/shard_map/jit(_where)/select_n | solution.py:55
  66.0 21.5 %select_n.33 = bf16[128,8192]{1,0:T(8,128)(2,1)} reshape(bf16[2,64,64,2,64]{4,3,2,1,0:T(2,128)(2,1)} %copy.62) | data formatting | bytes 4194304 | tf_op jit(solution)/shard_map/jit(_where)/select_n | solution.py:55
  88.3 1.2 pad_maximum_fusion.1
  89.4 2.4 gather_fusion
  91.9 2.7 fusion.4
  94.5 129.3 %all-to-all-done = bf16[64,2,64,256]{3,2,1,0:T(8,128)(2,1)} async-done(((bf16[64,2,64,256]{3,2,1,0:T(8,128)(2,1)}), bf16[64,2,64,256]{3,2,1,0:T(8,128)(2,1)}, u32[]{:S(2)}, u32[]{:S(2)}) %all-to-all-start) | async-done | bytes 4194336 | tf_op jit(solution)/shard_map/all_to_all | solution.py:67
  223.8 3.6 convolution_convert_fusion.2
  228.3 0.9 fusion.8
  229.3 31.5 %all-gather.3.cloned.1.call-done = bf16[2048,256]{1,0:T(8,128)(2,1)} async-done(((bf16[256,256]{1,0:T(8,128)(2,1)}), bf16[2048,256]{1,0:T(8,128)(2,1)}) %all-gather.3.cloned.1.call-update) | async-done | bytes 1048592 | tf_op jit(solution)/shard_map/all_gather | solution.py:86
  260.8 1.4 reduce_sum.12
  262.3 2.6 collective-permute-start.2
  265.0 4.9 collective-permute-done.2
  269.9 4.0 collective-permute-start.3
  274.5 3.7 collective-permute-done.3
  278.9 3.5 collective-permute-start.4
  283.6 2.3 collective-permute-done.4
  285.9 1.1 fusion.20
  287.7 1.1 pad_maximum_fusion
  288.8 2.5 copy.67
  291.3 1.4 fusion.9
  292.7 1.0 copy-done.2
  293.7 46.9 %custom-call.17 = f32[4,128,128]{2,1,0:T(8,128)S(1)} custom-call(f32[4,128,128]{2,1,0:T(8,128)S(1)} %cholesky.122), custom_call_target="Cholesky" | custom-call | tf_op jit(solution)/shard_map/jit(cholesky)/cholesky | solution.py:96
  340.6 1.1 cholesky.117
  341.7 0.7 select_bitcast_fusion
  342.5 39.3 %custom-call.18 = f32[4,1,128,128]{2,3,1,0:T(8,128)S(1)} custom-call(f32[4,1,128,128]{3,2,1,0:T(8,128)S(1)} %select_bitcast_fusion), custom_call_target="InvertDiagBlocksLowerTriangular" | custom-call | tf_op jit(solution)/shard_map/jit(cholesky)/cholesky | solution.py:96
  381.8 2.1 constant_dynamic-update-slice_fusion.1
  383.9 1.6 convolution_subtract_fusion.1
  385.5 46.9 %custom-call.19 = f32[4,128,128]{2,1,0:T(8,128)S(1)} custom-call(f32[4,128,128]{2,1,0:T(8,128)S(1)} %convolution_subtract_fusion.1), custom_call_target="Cholesky" | custom-call | tf_op jit(solution)/shard_map/jit(cholesky)/cholesky | solution.py:96
  432.4 0.8 select_reduce_fusion
  433.4 1.4 select_select_fusion
  434.9 0.9 copy-done.1
  436.5 5.4 %while.1 = (s32[]{:T(128)}, f32[3,256,256]{2,1,0:T(8,128)S(1)}, s32[2,2]{1,0:T(2,128)S(1)}, f32[2,3,128,128]{3,2,0,1:T(8,128)}, s32[]{:T(128)}) while((s32[]{:T(128)}, f32[3,256,256]{2,1,0:T(8,128)S(1)}, s32[2,2]{1,0:T(2,128)S(1)}, f32[2,3,128,128]{3,2,0,1:T(8,128)}, s32[]{:T(128)}) %tuple.36), condition=%wide.while_cond, body=%wide.while_body.sunk | while | flops 2 | bytes 394849 | solution.py:99
  437.1 2.1 bitcast_dynamic-update-slice_fusion.2
  439.8 2.1 bitcast_dynamic-update-slice_fusion.2
  441.9 60.4 %custom-call.20 = f32[3,2,128,128]{2,3,1,0:T(8,128)} custom-call(f32[3,2,128,128]{3,2,1,0:T(8,128)} %bitcast.103), custom_call_target="InvertDiagBlocksLowerTriangular" | custom-call | tf_op jit(solution)/shard_map/vmap(jit(_solve_triangular))/triangular_solve | solution.py:99
  502.3 1.7 fusion.31
  504.0 1.5 convolution_subtract_fusion
  506.0 0.9 copy.74
  506.9 1.8 copy.73
  (59 shorter events, 8.0 us)
Async XLA Ops:
  7.2 84.7 %copy-start = (bf16[2,10,256,256]{3,2,1,0:T(8,128)(2,1)S(1)}, bf16[2,10,256,256]{3,2,1,0:T(8,128)(2,1)}, u32[]{:S(2)}) copy-start(bf16[2,10,256,256]{3,2,1,0:T(8,128)(2,1)} %param.8) | copy-start | bytes 7864324
  14.9 19.0 %copy-start.5 = (bf16[512,256]{1,0:T(8,128)(2,1)S(1)}, bf16[512,256]{1,0:T(8,128)(2,1)}, u32[]{:S(2)}) copy-start(bf16[512,256]{1,0:T(8,128)(2,1)} %param.9) | copy-start | bytes 786436
  14.9 26.7 %copy-start.13 = (s32[2,10]{1,0:T(2,128)S(1)}, s32[2,10]{1,0:T(2,128)}, u32[]{:S(2)}) copy-start(s32[2,10]{1,0:T(2,128)} %param.10) | copy-start | bytes 244
  14.9 208.9 %all-to-all-start = ((bf16[64,2,64,256]{3,2,1,0:T(8,128)(2,1)}), bf16[64,2,64,256]{3,2,1,0:T(8,128)(2,1)}, u32[]{:S(2)}, u32[]{:S(2)}) async-start(bf16[64,2,64,256]{3,2,1,0:T(8,128)(2,1)} %copy.64), calls=%async_computation | async-start | bytes 8388608 | tf_op jit(solution)/shard_map/all_to_all | solution.py:67
  33.9 226.9 %all-gather.3.cloned.1.call-start = ((), (), s32[]{:S(2)}) async-start(), calls=%async_computation.1 | async-start | bytes 1179648 | tf_op jit(solution)/shard_map/all_gather | solution.py:86
  33.9 53.6 %collective-permute-start = (bf16[512,256]{1,0:T(8,128)(2,1)S(1)}, bf16[512,256]{1,0:T(8,128)(2,1)S(1)}, u32[]{:S(2)}, u32[]{:S(2)}) collective-permute-start(bf16[512,256]{1,0:T(8,128)(2,1)S(1)} %copy-done.5), channel_id=1, source_target_pairs={{0,1},{1,2},{2,3},{3,4},{4,5},{5,6},{6,7},{7,8},{8,9},{9,10},{10,1... | collective-permute-start | bytes 786440 | tf_op jit(solution)/shard_map/ppermute | solution.py:16
  35.8 52.4 %collective-permute-start.1 = (bf16[512,256]{1,0:T(8,128)(2,1)S(1)}, bf16[512,256]{1,0:T(8,128)(2,1)}, u32[]{:S(2)}, u32[]{:S(2)}) collective-permute-start(bf16[512,256]{1,0:T(8,128)(2,1)S(1)} %copy-done.5), channel_id=1, source_target_pairs={{1,0},{2,1},{3,2},{4,3},{5,4},{6,5},{7,6},{8,7},{9,8},{10,9},{11,1... | collective-permute-start | bytes 786440 | tf_op jit(solution)/shard_map/ppermute | solution.py:17
  47.1 4.0 copy-start.12
  87.5 0.7 copy-start.10
  223.8 3.6 copy-start.11
  227.6 0.7 copy-start.9
  262.3 7.5 %collective-permute-start.2 = (bf16[256,256]{0,1:T(8,128)(2,1)S(1)}, bf16[256,256]{0,1:T(8,128)(2,1)S(1)}, u32[]{:S(2)}, u32[]{:S(2)}) collective-permute-start(bf16[256,256]{0,1:T(8,128)(2,1)S(1)} %fusion.16), channel_id=1, source_target_pairs={{0,8},{8,0},{16,24},{24,16},{32,40},{40,32},{48,56},{56,48},{64,72... | collective-permute-start | bytes 393224 | tf_op jit(solution)/shard_map/ppermute | solution.py:25
  269.8 8.4 %copy-start.4 = (bf16[256,256]{0,1:T(8,128)(2,1)}, bf16[256,256]{0,1:T(8,128)(2,1)S(1)}, u32[]{:S(2)}) copy-start(bf16[256,256]{0,1:T(8,128)(2,1)S(1)} %collective-permute-done.2) | copy-start | bytes 393220
  269.9 8.4 %collective-permute-start.3 = (bf16[256,256]{0,1:T(8,128)(2,1)S(1)}, bf16[256,256]{0,1:T(8,128)(2,1)S(1)}, u32[]{:S(2)}, u32[]{:S(2)}) collective-permute-start(bf16[256,256]{0,1:T(8,128)(2,1)S(1)} %get-tuple-element.44), channel_id=1, source_target_pairs={{0,16},{8,24},{16,0},{24,8},{32,48},{40,56},{48,32},{56,40},{64,80... | collective-permute-start | bytes 393224 | tf_op jit(solution)/shard_map/ppermute | solution.py:25
  278.3 0.6 copy-start.7
  278.9 7.0 %collective-permute-start.4 = (bf16[256,256]{0,1:T(8,128)(2,1)S(1)}, bf16[256,256]{0,1:T(8,128)(2,1)}, u32[]{:S(2)}, u32[]{:S(2)}) collective-permute-start(bf16[256,256]{0,1:T(8,128)(2,1)S(1)} %get-tuple-element.39), channel_id=1, source_target_pairs={{0,32},{8,40},{16,48},{24,56},{32,0},{40,8},{48,16},{56,24},{64,96... | collective-permute-start | bytes 393224 | tf_op jit(solution)/shard_map/ppermute | solution.py:25
  287.0 0.7 copy-start.3
  292.7 1.0 copy-start.2
  293.7 139.7 %copy-start.6 = (pred[256,256]{1,0:T(8,128)(4,1)S(1)}, pred[256,256]{1,0:T(8,128)(4,1)}, u32[]{:S(2)}) copy-start(pred[256,256]{1,0:T(8,128)(4,1)} %iota_compare_fusion) | copy-start | bytes 196612
  385.5 51.0 %copy-start.14 = (s32[2]{0:T(128)S(1)}, s32[2]{0:T(128)}, u32[]{:S(2)}) copy-start(s32[2]{0:T(128)} %iota_multiply_fusion) | copy-start | bytes 28
  434.8 1.0 copy-start.1
  502.3 3.2 copy-start.8
Sparse Core Ops, SparseCore 0:
  229.4 31.3 all-gather.2
